TPU v7x, 256 devices: a whole 4x4x8 slice. The times are simulated.
256 devices in a mesh: pole: 4 (over y), row: 8 (over z_lo, x), col: 8 (over z_hi, core).
Axes of the slice: x: 4, y: 4, z: 8 (z_hi: 4, z_lo: 2; z = z_hi * 2 + z_lo), core: 2. Of those that a mesh axis runs over, the one named last changes fastest.
Arguments:
- found_inverse: bfloat16 [4, 2, 8192, 8, 8, 128], P('pole', None, 'row', None, 'col'), may hold values from -0.125 to 0.125
- l_panel: bfloat16 [4, 2, 8192, 512], P('pole', None, ('row', 'col')), may hold values from -1.5 to 1.5
- block_pattern: int32 [64, 4], P(('row', 'col')), may hold values 0 or 1
- sup_widths: int32 [4], replicated, may hold values from 1 to 128, 320 in all
- diag_inverse: bfloat16 [4, 2, 512, 128], P('pole'), may hold values from -6 to 6
- pole_weights: float32 [4, 2], P('pole'), may hold values from -4 to 4
Outputs:
- density: float32 [512, 8192], P('col', 'row')
- diagonal: float32 [512, 128], replicated
Inputs may be any that keep to these rules, and one draw needn't show every extreme that they name: `sup_widths`: one supernode has exactly 128 columns.
All inputs are finite; a program needn't handle non-finite values. No bound on the sum of `block_pattern` on one device may be relied on, other than what follows from the above.
Results may differ from a plain program's by a relative error of at most 0.0003.
Values may be sent and summed in bfloat16 or wider, within the bound.
A program may use at most 128 MiB of HBM per device.

v0:
```python
import jax
import jax.numpy as jnp
from jax import lax
from jax.sharding import PartitionSpec as P


def contract(left, right):
    return jnp.einsum("jk,ij->ki", left, right, preferred_element_type=jnp.float32)


def pair_product(left, right):
    return jnp.einsum("ika,kbi->kab", left, right, precision=lax.Precision.HIGHEST)


def per_device(found_inverse, l_panel, block_pattern, sup_widths, diag_inverse, pole_weights):
    slot_width = diag_inverse.shape[-1]
    total_cols = l_panel.shape[-1]
    supernodes = total_cols // slot_width
    row_count = lax.axis_size("row")
    row_index = lax.axis_index("row")
    col_index = lax.axis_index("col")
    columns = jnp.arange(total_cols, dtype=jnp.int32)
    column_ok = columns % slot_width < jnp.repeat(sup_widths, slot_width)
    block_ok = jnp.repeat(block_pattern[0], slot_width) == 1
    masked = jnp.where(
        (column_ok & block_ok)[None, None, :], l_panel[0], jnp.zeros((), jnp.bfloat16)
    )
    column_rows = lax.all_gather(masked, "row", axis=1, tiled=True)
    own_rows = lax.all_gather(masked, "col", axis=1, tiled=True)
    local_rows = found_inverse.shape[2]
    inverse = found_inverse[0].reshape(2, local_rows, row_count * slot_width)
    part_real = contract(column_rows[1], inverse[1]) - contract(column_rows[0], inverse[0])
    part_imag = -(contract(column_rows[1], inverse[0]) + contract(column_rows[0], inverse[1]))
    w_real = pole_weights[0, 0]
    w_imag = pole_weights[0, 1]
    weighted = w_real * part_real - w_imag * part_imag
    part = lax.psum_scatter(weighted, "col", scatter_dimension=0, tiled=True)
    density = lax.psum(part, "pole")
    lifted = own_rows.astype(jnp.float32).reshape(2, local_rows, supernodes, slot_width)
    upper_real = part_real.reshape(supernodes, slot_width, local_rows)
    upper_imag = part_imag.reshape(supernodes, slot_width, local_rows)
    t_real = pair_product(lifted[0], upper_real) - pair_product(lifted[1], upper_imag)
    t_imag = pair_product(lifted[0], upper_imag) + pair_product(lifted[1], upper_real)
    lead_flag = ((row_index == 0) & (col_index == 0)).astype(jnp.float32)
    d_real = diag_inverse[0, 0].astype(jnp.float32).reshape(supernodes, slot_width, slot_width)
    d_imag = diag_inverse[0, 1].astype(jnp.float32).reshape(supernodes, slot_width, slot_width)
    local_term = lead_flag * (w_real * d_real - w_imag * d_imag) - (
        w_real * t_real - w_imag * t_imag
    )
    diagonal = lax.psum(local_term.reshape(total_cols, slot_width), ("pole", "row", "col"))
    return (density, diagonal)


def solution(mesh):
    in_specs = (
        P("pole", None, "row", None, "col", None),
        P("pole", None, ("row", "col"), None),
        P(("row", "col"), None),
        P(),
        P("pole", None, None, None),
        P("pole", None),
    )
    out_specs = (P("col", "row"), P())
    return jax.shard_map(
        per_device, mesh=mesh, in_specs=in_specs, out_specs=out_specs, check_vma=False
    )
```

profile of v0, /device:TPU:2, one launch (start us, length us, event | category | flops | bytes accessed | tf_op | source)
XLA Modules:
  0.0 457.6 jit_solution(11535285280863356408)
XLA Ops:
  7.9 0.7 fusion.25
  8.6 1.7 bitcast_select_fusion
  11.1 1.4 fusion.28
  12.5 3.8 fusion.26
  16.3 38.6 %all-gather.3.cloned.1.call-done = bf16[2,1024,512]{2,1,0:T(8,128)(2,1)} async-done(((bf16[2,128,512]{2,1,0:T(8,128)(2,1)}), bf16[2,1024,512]{2,1,0:T(8,128)(2,1)}) %all-gather.3.cloned.1.call-update) | async-done | bytes 2097168 | tf_op jit(solution)/shard_map/all_gather | solution.py:28
  54.9 2.7 fusion.2
  57.6 1.3 fusion
  59.2 1.3 fusion.12
  60.5 4.6 %multiply_subtract_fusion = (f32[512,1024]{1,0:T(8,128)}, f32[512,1024]{1,0:T(8,128)}) fusion(f32[512,1024]{1,0:T(8,128)S(1)} %fusion.12, f32[]{:T(128)} %bitcast.7, f32[]{:T(128)} %bitcast, f32[512,1024]{1,0:T(8,128)S(1)} %fusion, bf16[128,8,8,128]{3,2,1,0:T(8,128)(2,1)S(1)} %bitcast.67, bf16[2,1024,512]{2,1,0:T(8,128)(2,1)S(1)} %copy-done.3), kind=kOutput, calls=%fused_computation.8 | convolution fusion | flops 1076363264 | bytes 11534344 | tf_op jit(solution)/shard_map/jk,ij->ki/dot_general | solution.py:8
  65.2 0.9 copy-done.4
  66.1 1.3 subtract_multiply_fusion
  67.4 27.9 %all-gather.5.cloned.1.call-done = bf16[2,1024,512]{2,1,0:T(8,128)(2,1)} async-done(((bf16[2,128,512]{2,1,0:T(8,128)(2,1)}), bf16[2,1024,512]{2,1,0:T(8,128)(2,1)}) %all-gather.5.cloned.1.call-update) | async-done | bytes 2097168 | tf_op jit(solution)/shard_map/all_gather | solution.py:29
  95.3 2.7 fusion.27
  97.9 1.3 copy.8
  99.3 1.5 copy.9
  100.8 2.5 fusion.29
  103.3 1.2 fusion.30
  104.5 1.9 fusion.20
  106.4 2.5 fusion.19
  109.0 31.0 %reduce-scatter.2.cloned.1.call-done = f32[64,1024]{1,0:T(8,128)} async-done(((f32[512,1024]{1,0:T(8,128)}), f32[64,1024]{1,0:T(8,128)}) %reduce-scatter.2.cloned.1.call-update) | async-done | bytes 262160 | tf_op jit(solution)/shard_map/reduce_scatter | solution.py:37
  140.1 259.7 %all-reduce.5.cloned.1.call-done = f32[512,128]{1,0:T(8,128)} async-done(((f32[512,128]{1,0:T(8,128)}), f32[512,128]{1,0:T(8,128)}) %all-reduce.5.cloned.1.call-update) | async-done | bytes 262160 | tf_op jit(solution)/shard_map/psum | solution.py:50
  399.8 48.0 %all-reduce.3.cloned.1.call-done = f32[64,1024]{1,0:T(8,128)} async-done(((f32[64,1024]{1,0:T(8,128)}), f32[64,1024]{1,0:T(8,128)}) %all-reduce.3.cloned.1.call-update) | async-done | bytes 262160 | tf_op jit(solution)/shard_map/psum | solution.py:38
  447.8 1.7 copy.36
  449.4 1.7 copy.37
  (20 shorter events, 1.9 us)
Async XLA Ops:
  7.2 47.7 %all-gather.3.cloned.1.call-start = ((), (), s32[]{:S(2)}) async-start(), calls=%async_computation.1 | async-start | bytes 2359296 | tf_op jit(solution)/shard_map/all_gather | solution.py:28
  10.3 85.0 %all-gather.5.cloned.1.call-start = ((), (), s32[]{:S(2)}) async-start(), calls=%async_computation.4 | async-start | bytes 2359296 | tf_op jit(solution)/shard_map/all_gather | solution.py:29
  11.1 129.0 %reduce-scatter.2.cloned.1.call-start = ((), (), s32[]{:S(2)}) async-start(), calls=%async_computation.2 | async-start | bytes 2359296 | tf_op jit(solution)/shard_map/reduce_scatter | solution.py:37
  54.9 2.7 copy-start.3
  57.6 1.6 copy-start.2
  65.1 0.9 copy-start.4
  65.1 334.7 %all-reduce.5.cloned.1.call-start = ((), (), s32[]{:S(2)}) async-start(), calls=%async_computation.5 | async-start | bytes 524288 | tf_op jit(solution)/shard_map/psum | solution.py:50
  100.8 2.6 copy-start
  100.8 2.6 copy-start.1
  108.9 338.8 %all-reduce.3.cloned.1.call-start = ((), (), s32[]{:S(2)}) async-start(), calls=%async_computation.3 | async-start | bytes 524288 | tf_op jit(solution)/shard_map/psum | solution.py:38
Sparse Core Ops, SparseCore 0:
  10.4 44.4 all-gather.2
  57.3 37.9 all-gather.4
  97.8 42.1 reduce-scatter.1
  145.9 253.8 all-reduce.4
  402.0 45.7 all-reduce.2
where the time goes:
time: 458 us
  waiting for transfers between devices  406 us (89%)
  matrix products  18 us (4%)
  local copies, waits for them, and re-layouts  15.2 us (3%)
  between operations  13.9 us (3%)
    psum x1, waiting for transfers between devices, per_device(): lax.psum(local_term.reshape(total_cols, slot_width), ('pole', 'row', 'col'))  260 us
    psum x1, waiting for transfers between devices, per_device(): density = lax.psum(part, 'pole')  48 us
    all_gather x1, waiting for transfers between devices, per_device(): column_rows = lax.all_gather(masked, 'row', axis=1, tiled=True)  38.6 us
    reduce_scatter x1, waiting for transfers between devices, per_device(): part = lax.psum_scatter(weighted, 'col', scatter_dimension=0, tiled=True)  31 us
    all_gather x1, waiting for transfers between devices, per_device(): own_rows = lax.all_gather(masked, 'col', axis=1, tiled=True)  27.9 us
    dot_general x4, matrix products, contract(): jnp.einsum('jk,ij->ki', left, right, preferred_element_type=jnp.float32)  9.92 us
  transfers between devices with their start and end apart: 5, of which 5 were waited for; matrix products, arithmetic and copies ran while one was open for 7% of the time, Pallas kernels for 0%

commit v1 on v0

--- a/solution.py
+++ b/solution.py
@@ -35,7 +35,11 @@
     w_imag = pole_weights[0, 1]
     weighted = w_real * part_real - w_imag * part_imag
     part = lax.psum_scatter(weighted, "col", scatter_dimension=0, tiled=True)
-    density = lax.psum(part, "pole")
+    count = lax.axis_size("pole")
+    density, far = (part, 1)
+    while far < count:
+        density = density + lax.ppermute(density, "pole", [(i, i ^ far) for i in range(count)])
+        far = 2 * far
     lifted = own_rows.astype(jnp.float32).reshape(2, local_rows, supernodes, slot_width)
     upper_real = part_real.reshape(supernodes, slot_width, local_rows)
     upper_imag = part_imag.reshape(supernodes, slot_width, local_rows)

time: 458 us -> 414 us (0.904)
  waiting for transfers between devices: 406 us -> 353 us
    psum x1 -> x0, waiting for transfers between devices: 48 us -> none  [per_device(): density = lax.psum(part, 'pole')]
    psum x1, waiting for transfers between devices: 260 us -> 248 us  [per_device(): lax.psum(local_term.reshape(total_cols, slot_width), ('pole', 'row', 'col'))]
  transfers between devices with their start and end apart: 5 -> 6, of which waited for: 5 -> 6; matrix products, arithmetic and copies ran while one was open for 7% -> 9% of each run, Pallas kernels for 0% -> 0%
where the time goes in v1:
time: 414 us; the launch traced here: 413 us
  waiting for transfers between devices  353 us (85%)
  matrix products  20.8 us (5%)
  between operations  13.9 us (3%)
  local copies, waits for them, and re-layouts  13.5 us (3%)
  other arithmetic  6.84 us (2%)
  starting transfers between devices  4.66 us (1%)
    psum x1, waiting for transfers between devices, per_device(): lax.psum(local_term.reshape(total_cols, slot_width), ('pole', 'row', 'col'))  248 us
    all_gather x1, waiting for transfers between devices, per_device(): column_rows = lax.all_gather(masked, 'row', axis=1, tiled=True)  38.5 us
    reduce_scatter x1, waiting for transfers between devices, per_device(): part = lax.psum_scatter(weighted, 'col', scatter_dimension=0, tiled=True)  34.5 us
    all_gather x1, waiting for transfers between devices, per_device(): own_rows = lax.all_gather(masked, 'col', axis=1, tiled=True)  27 us
    dot_general x4, matrix products, pair_product(): jnp.einsum('ika,kbi->kab', left, right, precision=lax.Precision.HIGHEST)  10.8 us
    dot_general x4, matrix products, contract(): jnp.einsum('jk,ij->ki', left, right, preferred_element_type=jnp.float32)  10 us
  transfers between devices with their start and end apart: 6, of which 6 were waited for; matrix products, arithmetic and copies ran while one was open for 9% of the time, Pallas kernels for 0%

profile of v1, /device:TPU:2, one launch (start us, length us, event | category | flops | bytes accessed | tf_op | source)
XLA Modules:
  0.0 413.1 jit_solution(10683828812928990843)
XLA Ops:
  8.6 1.7 bitcast_select_fusion
  11.1 1.4 fusion.28
  12.5 3.9 fusion.26
  16.3 38.5 %all-gather.3.cloned.1.call-done = bf16[2,1024,512]{2,1,0:T(8,128)(2,1)} async-done(((bf16[2,128,512]{2,1,0:T(8,128)(2,1)}), bf16[2,1024,512]{2,1,0:T(8,128)(2,1)}) %all-gather.3.cloned.1.call-update) | async-done | bytes 2097168 | tf_op jit(solution)/shard_map/all_gather | solution.py:28
  54.9 2.7 fusion.2
  57.6 1.3 fusion
  60.5 4.8 %multiply_subtract_fusion = (f32[512,1024]{1,0:T(8,128)}, f32[512,1024]{1,0:T(8,128)}) fusion(f32[512,1024]{1,0:T(8,128)S(1)} %fusion.12, f32[]{:T(128)} %bitcast.7, f32[]{:T(128)} %bitcast, f32[512,1024]{1,0:T(8,128)S(1)} %fusion, bf16[128,8,8,128]{3,2,1,0:T(8,128)(2,1)S(1)} %bitcast.67, bf16[2,1024,512]{2,1,0:T(8,128)(2,1)S(1)} %copy-done.4), kind=kOutput, calls=%fused_computation.8 | convolution fusion | flops 1076363264 | bytes 11534344 | tf_op jit(solution)/shard_map/jk,ij->ki/dot_general | solution.py:8
  66.2 2.1 subtract_multiply_fusion
  68.2 27.0 %all-gather.5.cloned.1.call-done = bf16[2,1024,512]{2,1,0:T(8,128)(2,1)} async-done(((bf16[2,128,512]{2,1,0:T(8,128)(2,1)}), bf16[2,1024,512]{2,1,0:T(8,128)(2,1)}) %all-gather.5.cloned.1.call-update) | async-done | bytes 2097168 | tf_op jit(solution)/shard_map/all_gather | solution.py:29
  95.3 2.7 fusion.27
  97.9 1.3 copy.8
  99.2 1.5 copy.9
  100.7 2.5 fusion.29
  103.3 2.5 fusion.20
  105.8 34.5 %reduce-scatter.2.cloned.1.call-done = f32[64,1024]{1,0:T(8,128)} async-done(((f32[512,1024]{1,0:T(8,128)}), f32[64,1024]{1,0:T(8,128)}) %reduce-scatter.2.cloned.1.call-update) | async-done | bytes 262160 | tf_op jit(solution)/shard_map/reduce_scatter | solution.py:37
  140.3 1.3 collective-permute-start
  141.6 3.1 fusion.30
  144.7 2.2 collective-permute-done
  146.9 3.2 collective-permute-start.1
  150.1 2.6 fusion.19
  152.7 2.3 collective-permute-done.1
  155.0 1.7 add.29
  156.7 248.2 %all-reduce.2.cloned.1.call-done = f32[512,128]{1,0:T(8,128)} async-done(((f32[512,128]{1,0:T(8,128)}), f32[512,128]{1,0:T(8,128)}) %all-reduce.2.cloned.1.call-update) | async-done | bytes 262160 | tf_op jit(solution)/shard_map/psum | solution.py:54
  404.9 1.7 copy.35
  (26 shorter events, 4.8 us)
Async XLA Ops:
  7.2 47.7 %all-gather.3.cloned.1.call-start = ((), (), s32[]{:S(2)}) async-start(), calls=%async_computation.1 | async-start | bytes 2359296 | tf_op jit(solution)/shard_map/all_gather | solution.py:28
  10.3 85.0 %all-gather.5.cloned.1.call-start = ((), (), s32[]{:S(2)}) async-start(), calls=%async_computation.3 | async-start | bytes 2359296 | tf_op jit(solution)/shard_map/all_gather | solution.py:29
  11.1 129.3 %reduce-scatter.2.cloned.1.call-start = ((), (), s32[]{:S(2)}) async-start(), calls=%async_computation.2 | async-start | bytes 2359296 | tf_op jit(solution)/shard_map/reduce_scatter | solution.py:37
  54.9 2.7 copy-start.4
  57.6 1.6 copy-start.1
  65.2 0.9 copy-start.6
  65.3 339.7 %all-reduce.2.cloned.1.call-start = ((), (), s32[]{:S(2)}) async-start(), calls=%async_computation.4 | async-start | bytes 524288 | tf_op jit(solution)/shard_map/psum | solution.py:54
  100.7 2.6 copy-start
  140.3 6.6 %copy-start.5 = (f32[64,1024]{1,0:T(8,128)S(1)}, f32[64,1024]{1,0:T(8,128)}, u32[]{:S(2)}) copy-start(f32[64,1024]{1,0:T(8,128)} %reduce-scatter.2.cloned.1.call-done) | copy-start | bytes 786436
  140.3 9.8 %copy-start.2 = (f32[1,1,512,128]{3,2,1,0:T(8,128)S(1)}, f32[1,1,512,128]{3,2,1,0:T(8,128)}, u32[]{:S(2)}) copy-start(f32[1,1,512,128]{3,2,1,0:T(8,128)} %subtract_multiply_fusion) | copy-start | bytes 786436
  140.3 9.8 %copy-start.3 = (f32[4,128,128]{2,1,0:T(8,128)S(1)}, f32[4,128,128]{2,1,0:T(8,128)}, u32[]{:S(2)}) copy-start(f32[4,128,128]{2,1,0:T(8,128)} %fusion.20) | copy-start | bytes 786436
  140.3 6.6 %collective-permute-start = (f32[64,1024]{1,0:T(8,128)}, f32[64,1024]{1,0:T(8,128)S(1)}, u32[]{:S(2)}, u32[]{:S(2)}) collective-permute-start(f32[64,1024]{1,0:T(8,128)} %reduce-scatter.2.cloned.1.call-done), channel_id=1, source_target_pairs={{0,64},{64,0},{128,192},{192,128},{1,65},{65,1},{129,193},{193,129... | collective-permute-start | bytes 786440 | tf_op jit(solution)/shard_map/ppermute | solution.py:41
  146.9 8.1 %collective-permute-start.1 = (f32[64,1024]{1,0:T(8,128)S(1)}, f32[64,1024]{1,0:T(8,128)}, u32[]{:S(2)}, u32[]{:S(2)}) collective-permute-start(f32[64,1024]{1,0:T(8,128)S(1)} %add.28), channel_id=1, source_target_pairs={{0,128},{64,192},{128,0},{192,64},{1,129},{65,193},{129,1},{193,65... | collective-permute-start | bytes 786440 | tf_op jit(solution)/shard_map/ppermute | solution.py:41
Sparse Core Ops, SparseCore 0:
  10.4 44.4 all-gather.2
  57.3 37.9 all-gather.4
  97.8 42.4 reduce-scatter.1
  152.8 252.0 all-reduce.1
